TPU v7x, 512 devices: a whole 4x4x16 slice. The times are simulated.
512 devices in a mesh: rows: 64 (over z, y), cols: 8 (over x, core).
Axes of the slice: x: 4, y: 4, z: 16, core: 2. Of those that a mesh axis runs over, the one named last changes fastest.
Arguments:
- x_start: float32 [96, 32768], P('cols', 'rows'), may hold values from -6 to 6
- p_start: float32 [96, 32768], P('cols', 'rows'), may hold values from -6 to 6
- k_diag: bfloat16 [512, 64, 64], P('rows'), as said below
- k_link: bfloat16 [512, 4, 64, 64], P('rows')
- m_diag: bfloat16 [512, 64, 64], P('rows'), as said below
- m_link: bfloat16 [512, 4, 64, 64], P('rows')
- link_to: int32 [512, 4], P('rows'), may hold values from 0 to 7, as said below
- link_count: int32 [512], P('rows'), may hold values from 1 to 4, as said below
- k_iface: bfloat16 [64, 64, 3, 64, 64], P('rows'), as said below
- m_iface: bfloat16 [64, 64, 3, 64, 64], P('rows'), as said below
- iface_local: int32 [64, 64, 3], P('rows'), may hold values from 0 to 7, as said below
- iface_live: int32 [64, 64, 3], P('rows'), may hold values from 0 to 1, as said below
Outputs:
- x_out: float32 [96, 32768], P('cols', 'rows')
- p_out: float32 [96, 32768], P('cols', 'rows')
- ritz: float32 [96, 96], replicated
Inputs may be any that keep to these rules, and one draw needn't show every extreme that they name: `link_to`: for each row owner and each b < 4, the b-th links of its 8 supernodes form a permutation of its supernodes. `link_count`: the first supernode of every row owner has all 4 links live. `iface_local`: each row owner's 192 slots name each of its supernodes at most (199) // 8 times. iface_live[p, q, c] = iface_live[q, p, c], and it is 0 where p = q. `k_iface`: for p < q the block for (q, p, c) is the transpose of the block for (p, q, c). `m_iface`: for p < q the block for (q, p, c) is the transpose of the block for (p, q, c). `k_diag`: every block is symmetric with diagonal entries of 1 or more. `m_diag`: every block is symmetric with diagonal entries of 1 or more.
All inputs are finite; a program needn't handle non-finite values.
Results may differ from a plain program's by a relative error of at most 0.0003.
Values sent between devices are 32-bit elements; how exact they have to be, the bound alone decides.
No kernel may reach another device: no remote copies, remote signals or barrier semaphores. Data moves between devices by JAX's collectives and lax.ppermute only.
A program may use at most 128 MiB of HBM per device.

v0:
```python
import jax
import jax.numpy as jnp
from jax import lax
from jax.sharding import PartitionSpec as P

STEPS = 2
RR_ITERS = 3
exact_dots = lax.Precision.HIGHEST


def symmetric(matrix):
    return 0.5 * (matrix + matrix.T)


def local_product(vectors, diag_blocks, link_blocks, link_onehot, link_live):
    near = (
        jnp.einsum("sbt,ctj->csbj", link_onehot, vectors, precision=exact_dots)
        * link_live[None, :, :, None]
    )
    result = jnp.einsum(
        "sij,csj->csi", diag_blocks.astype(jnp.float32), vectors, precision=exact_dots
    )
    result = result + jnp.einsum(
        "sbij,csbj->csi", link_blocks.astype(jnp.float32), near, precision=exact_dots
    )
    back = (
        jnp.einsum("sbji,csj->csbi", link_blocks.astype(jnp.float32), vectors, precision=exact_dots)
        * link_live[None, :, :, None]
    )
    return result + jnp.einsum("sbt,csbi->cti", link_onehot, back, precision=exact_dots)


def apply_pair(vectors, tables):
    (
        k_diag,
        k_link,
        m_diag,
        m_link,
        link_onehot,
        link_live,
        k_faces,
        m_faces,
        slot_onehot,
        slot_live,
    ) = tables
    col_count, row_count = vectors.shape
    node_count = link_onehot.shape[0]
    node_size = k_diag.shape[1]
    split_vec = vectors.reshape(col_count, node_count, node_size)
    picked = jnp.einsum("ks,csj->kcj", slot_onehot, split_vec, precision=exact_dots)
    owners = lax.axis_size("rows")

    def face_term(faces):
        term = (
            jnp.einsum("kij,kcj->kci", faces.astype(jnp.float32), picked, precision=exact_dots)
            * slot_live[:, None, None]
        )
        return term.reshape(owners, -1)

    recv_k, recv_m = (
        lax.all_to_all(face_term(k_faces), "rows", split_axis=0, concat_axis=0, tiled=True),
        lax.all_to_all(face_term(m_faces), "rows", split_axis=0, concat_axis=0, tiled=True),
    )

    def finish(diag_blocks, link_blocks, received):
        local = local_product(split_vec, diag_blocks, link_blocks, link_onehot, link_live)
        arrived = jnp.einsum(
            "ks,kci->csi",
            slot_onehot,
            received.reshape(-1, col_count, node_size),
            precision=exact_dots,
        )
        return (local + arrived).reshape(col_count, row_count)

    return (finish(k_diag, k_link, recv_k), finish(m_diag, m_link, recv_m))


def gram_pair(own_s, own_k, own_m):
    blocks, col_part, row_count = own_s.shape
    modes = col_part * lax.axis_size("cols")
    dof_count = row_count * lax.axis_size("rows")
    empty = jnp.zeros((blocks, modes, blocks, col_part), jnp.float32)
    panel_rows = lax.all_gather(own_s, "cols", axis=1, tiled=True)
    offset = jnp.int32(0)
    term_k = jnp.einsum("anr,bcr->anbc", panel_rows, own_k, precision=exact_dots)
    term_m = jnp.einsum("anr,bcr->anbc", panel_rows, own_m, precision=exact_dots)
    part_k = lax.dynamic_update_slice_in_dim(empty, term_k, offset, 1)
    part_m = lax.dynamic_update_slice_in_dim(empty, term_m, offset, 1)
    summed_k, summed_m = lax.psum((part_k, part_m), "rows")
    full_k, full_m = (
        lax.all_gather(summed_k, "cols", axis=3, tiled=True),
        lax.all_gather(summed_m, "cols", axis=3, tiled=True),
    )
    extent = blocks * modes
    return (
        symmetric(full_k.reshape(extent, extent) / dof_count),
        symmetric(full_m.reshape(extent, extent) / dof_count),
        own_s,
    )


def rayleigh(gram_stiff, gram_mass, modes):
    total = gram_stiff.shape[0]
    factor = jnp.linalg.cholesky(gram_stiff)
    coeffs = jnp.eye(total, modes, dtype=jnp.float32)
    for inner_index in range(RR_ITERS):
        solved = jax.scipy.linalg.cho_solve(
            (factor, True), jnp.dot(gram_mass, coeffs, precision=exact_dots)
        )
        inner = symmetric(
            jnp.dot(
                solved.T, jnp.dot(gram_mass, solved, precision=exact_dots), precision=exact_dots
            )
        )
        inner_factor = jnp.linalg.cholesky(inner)
        coeffs = jax.scipy.linalg.solve_triangular(inner_factor, solved.T, lower=True).T
    ritz_new = symmetric(
        jnp.dot(coeffs.T, jnp.dot(gram_stiff, coeffs, precision=exact_dots), precision=exact_dots)
    )
    return (coeffs, ritz_new)


def contract(coef, panel_rows):
    new_x = jnp.einsum("anc,anr->cr", coef, panel_rows, precision=exact_dots)
    new_p = jnp.einsum("anc,anr->cr", coef[1:], panel_rows[1:], precision=exact_dots)
    return (new_x, new_p)


def own_columns(coeffs, blocks, col_part):
    modes = coeffs.shape[1]
    col_start = lax.axis_index("cols") * col_part
    return lax.dynamic_slice_in_dim(coeffs.reshape(blocks, modes, modes), col_start, col_part, 2)


def mass_mixture(mass_x, ritz_now):
    col_part, row_count = mass_x.shape
    col_start = lax.axis_index("cols") * col_part
    coef = lax.dynamic_slice_in_dim(ritz_now, col_start, col_part, 1)
    panel_rows = lax.all_gather(mass_x, "cols", axis=0, tiled=True)
    part = lax.slice_in_dim(coef, 0, panel_rows.shape[0], axis=0)
    return jnp.zeros((col_part, row_count), jnp.float32) + jnp.einsum(
        "nc,nr->cr", part, panel_rows, precision=exact_dots
    )


def body(
    x_start,
    p_start,
    k_diag,
    k_link,
    m_diag,
    m_link,
    link_to,
    link_count,
    k_iface,
    m_iface,
    iface_local,
    iface_live,
):
    col_part, row_count = x_start.shape
    modes = col_part * lax.axis_size("cols")
    node_count, link_slots = link_to.shape
    node_size = k_diag.shape[1]
    node_ids = jnp.arange(node_count, dtype=jnp.int32)
    link_onehot = (link_to[:, :, None] == node_ids[None, None, :]).astype(jnp.float32)
    link_live = (jnp.arange(link_slots, dtype=jnp.int32)[None, :] < link_count[:, None]).astype(
        jnp.float32
    )
    local_slots = iface_local.reshape(-1)
    slot_onehot = (local_slots[:, None] == node_ids[None, :]).astype(jnp.float32)
    slot_live = iface_live.reshape(-1).astype(jnp.float32)
    k_faces = k_iface.reshape(-1, node_size, node_size)
    m_faces = m_iface.reshape(-1, node_size, node_size)
    tables = (
        k_diag,
        k_link,
        m_diag,
        m_link,
        link_onehot,
        link_live,
        k_faces,
        m_faces,
        slot_onehot,
        slot_live,
    )
    precond = 1.0 / jnp.diagonal(k_diag.astype(jnp.float32), axis1=1, axis2=2).reshape(-1)
    both_k, both_m = apply_pair(jnp.concatenate([x_start, p_start], 0), tables)
    stiff_x, stiff_p = (both_k[:col_part], both_k[col_part:])
    mass_x, mass_p = (both_m[:col_part], both_m[col_part:])
    x_block, p_block = (x_start, p_start)
    stiff_gram, mass_gram, unused = gram_pair(x_block[None], stiff_x[None], mass_x[None])
    ritz_now = jax.scipy.linalg.cho_solve((jnp.linalg.cholesky(mass_gram), True), stiff_gram)
    for step_index in range(STEPS):
        resid = stiff_x - mass_mixture(mass_x, ritz_now)
        search = resid * precond[None, :]
        stiff_w, mass_w = apply_pair(search, tables)
        own_s = jnp.stack([x_block, search, p_block], 0)
        own_k = jnp.stack([stiff_x, stiff_w, stiff_p], 0)
        own_m = jnp.stack([mass_x, mass_w, mass_p], 0)
        gram_stiff, gram_mass, whole = gram_pair(own_s, own_k, own_m)
        coeffs, ritz_new = rayleigh(gram_stiff, gram_mass, modes)
        mine = own_columns(coeffs, 3, col_part)
        empty = jnp.zeros((col_part, row_count), jnp.float32)
        panel_rows = lax.all_gather(own_s, "cols", axis=1, tiled=True)
        add_coef = lax.slice_in_dim(mine, 0, panel_rows.shape[1], axis=1)
        new_x, new_p = contract(add_coef, panel_rows)
        x_block = empty + new_x
        p_block = empty + new_p
        if step_index + 1 < STEPS:
            blank = jnp.zeros((col_part, row_count), jnp.float32)
            panels = (
                lax.all_gather(own_k, "cols", axis=1, tiled=True),
                lax.all_gather(own_m, "cols", axis=1, tiled=True),
            )
            coef = lax.slice_in_dim(mine, 0, panels[0].shape[1], axis=1)
            new_kx, new_kp = contract(coef, panels[0])
            new_mx, new_mp = contract(coef, panels[1])
            stiff_x = blank + new_kx
            stiff_p = blank + new_kp
            mass_x = blank + new_mx
            mass_p = blank + new_mp
        ritz_now = ritz_new
    return (x_block, p_block, ritz_now)


def solution(mesh):
    placed = (
        P("cols", "rows"),
        P("cols", "rows"),
        P("rows", None, None),
        P("rows", None, None, None),
        P("rows", None, None),
        P("rows", None, None, None),
        P("rows", None),
        P("rows"),
        P("rows", None, None, None, None),
        P("rows", None, None, None, None),
        P("rows", None, None),
        P("rows", None, None),
    )
    return jax.shard_map(
        body,
        mesh=mesh,
        in_specs=placed,
        out_specs=(P("cols", "rows"), P("cols", "rows"), P()),
        check_vma=False,
    )
```

profile of v0, /device:TPU:1, one launch (start us, length us, event | category | flops | bytes accessed | tf_op | source)
XLA Modules:
  0.0 1823.3 jit_solution(2422586496049059222)
XLA Ops:
  14.4 9.0 convolution_multiply_fusion
  23.4 3.7 all_to_all.49
  27.0 19.5 %all-to-all-start.1 = ((f32[64,1,4608]{2,1,0:T(1,128)}), f32[64,1,4608]{2,1,0:T(1,128)}, u32[]{:S(2)}, u32[]{:S(2)}) async-start(f32[64,1,4608]{2,1,0:T(1,128)} %all_to_all.49), calls=%async_computation.1 | async-start | bytes 2359296 | tf_op jit(solution)/shard_map/all_to_all | solution.py:62
  46.6 7.4 convolution_multiply_fusion.1
  54.0 3.7 all_to_all.48
  57.7 45.7 %all-to-all-done.1 = f32[64,1,4608]{2,1,0:T(1,128)} async-done(((f32[64,1,4608]{2,1,0:T(1,128)}), f32[64,1,4608]{2,1,0:T(1,128)}, u32[]{:S(2)}, u32[]{:S(2)}) %all-to-all-start.1) | async-done | bytes 1179680 | tf_op jit(solution)/shard_map/all_to_all | solution.py:62
  103.3 9.9 all-to-all-start
  114.1 15.6 all-gather.1
  141.7 5.1 reduce.17
  157.5 11.7 all-to-all-done
  169.2 5.1 reduce.16
  183.8 222.6 %all-reduce.5 = (f32[1,96,1,12]{1,3,2,0:T(8,128)S(1)}, f32[1,96,1,12]{1,3,2,0:T(8,128)S(1)}) all-reduce(f32[1,96,1,12]{1,3,2,0:T(8,128)S(1)} %convolution_bitcast_fusion.19, f32[1,96,1,12]{1,3,2,0:T(8,128)S(1)} %convolution_bitcast_fusion.20), channel_id=1, replica_groups=mesh['rows'=64,'cols'=8] {'rows'}, use_global_device_ids=true, to_apply=%region_3.5 | all-reduce | flops 2304 | bytes 18432 | tf_op jit(solution)/shard_map/psum | solution.py:89
  406.3 71.9 %all_gather.42 = f32[1,96,1,96]{1,2,0,3:T(1,128)S(1)} all-gather(f32[1,96,1,12]{1,2,0,3:T(1,128)S(1)} %copy.371), channel_id=1, replica_groups=mesh['rows'=64,'cols'=8] {'cols'}, dimensions={3}, use_global_device_ids=true | all-gather | bytes 41472 | tf_op jit(solution)/shard_map/all_gather | solution.py:92
  478.6 8.8 cholesky.329
  488.7 7.4 custom-call.31
  496.1 12.8 all_gather.43
  510.2 12.8 all-gather.2
  529.5 7.6 convolution_multiply_fusion.5
  540.0 6.5 all-to-all-start.2
  548.3 8.5 convolution_multiply_fusion.4
  562.8 17.3 all-to-all-done.2
  580.1 7.5 all-to-all-start.3
  599.7 16.2 all_gather.45
  615.9 3.3 reduce.18
  629.2 3.3 reduce.19
  642.4 14.5 all_gather.48
  656.9 13.4 all_gather.49
  673.4 234.2 %all-reduce.11.cloned.1.call-done = (f32[3,96,3,12]{1,3,2,0:T(8,128)}, f32[3,96,3,12]{1,3,2,0:T(8,128)}) async-done(((f32[3,96,3,12]{1,3,2,0:T(8,128)}, f32[3,96,3,12]{1,3,2,0:T(8,128)}), (f32[3,96,3,12]{1,3,2,0:T(8,128)}, f32[3,96,3,12]{1,3,2,0:T(8,128)})) %all-reduce.11.cloned.1.call-update) | async-done | bytes 82960 | tf_op jit(solution)/shard_map/psum | solution.py:89
  908.5 25.0 %all_gather.46 = f32[3,96,3,96]{1,2,0,3:T(4,128)} all-gather(f32[3,96,3,12]{1,2,0,3:T(4,128)S(1)} %copy.399), channel_id=1, replica_groups=mesh['rows'=64,'cols'=8] {'cols'}, dimensions={3}, use_global_device_ids=true | all-gather | bytes 373248 | tf_op jit(solution)/shard_map/all_gather | solution.py:91
  947.7 11.7 cholesky.342
  960.3 9.8 custom-call.46
  973.0 11.7 cholesky.361
  985.4 10.2 custom-call.47
  1006.0 5.8 while.12
  1012.4 29.5 %custom-call.52 = f32[3,128,128]{1,2,0:T(8,128)S(1)} custom-call(f32[3,128,128]{2,1,0:T(8,128)S(1)} %pad_maximum_fusion), custom_call_target="InvertDiagBlocksLowerTriangular" | custom-call | tf_op jit(solution)/shard_map/jit(_cho_solve)/triangular_solve | solution.py:107
  1042.8 14.3 all_gather.47
  1079.9 9.6 cholesky.397
  1091.4 8.2 custom-call.49
  1113.7 9.7 cholesky.408
  1125.3 8.2 custom-call.51
  1143.6 8.8 cholesky.419
  1153.7 7.4 custom-call.53
  1170.4 13.0 all-gather.3
  1190.5 7.5 convolution_multiply_fusion.3
  1201.1 9.1 all-to-all-start.4
  1212.3 8.5 convolution_multiply_fusion.2
  1228.7 15.0 all-to-all-done.4
  1243.7 7.5 all-to-all-start.5
  1262.0 15.7 all_gather.51
  1304.6 248.9 %all-reduce.9.cloned.1.call-done = (f32[3,96,3,12]{1,3,2,0:T(8,128)}, f32[3,96,3,12]{1,3,2,0:T(8,128)}) async-done(((f32[3,96,3,12]{1,3,2,0:T(8,128)}, f32[3,96,3,12]{1,3,2,0:T(8,128)}), (f32[3,96,3,12]{1,3,2,0:T(8,128)}, f32[3,96,3,12]{1,3,2,0:T(8,128)})) %all-reduce.9.cloned.1.call-update) | async-done | bytes 82960 | tf_op jit(solution)/shard_map/psum | solution.py:89
  1554.4 25.0 %all_gather.52 = f32[3,96,3,96]{1,2,0,3:T(4,128)} all-gather(f32[3,96,3,12]{1,2,0,3:T(4,128)S(1)} %copy.458), channel_id=1, replica_groups=mesh['rows'=64,'cols'=8] {'cols'}, dimensions={3}, use_global_device_ids=true | all-gather | bytes 373248 | tf_op jit(solution)/shard_map/all_gather | solution.py:91
  1593.6 11.7 cholesky.432
  1606.1 9.8 custom-call.54
  1618.9 11.7 cholesky.451
  1632.5 10.1 custom-call.55
  1652.4 5.8 while.13
  1658.3 29.5 %custom-call.60 = f32[3,128,128]{1,2,0:T(8,128)S(1)} custom-call(f32[3,128,128]{2,1,0:T(8,128)S(1)} %pad_maximum_fusion.1), custom_call_target="InvertDiagBlocksLowerTriangular" | custom-call | tf_op jit(solution)/shard_map/jit(_cho_solve)/triangular_solve | solution.py:107
  1688.7 14.3 all_gather.53
  1725.8 9.6 cholesky.487
  1737.4 8.2 custom-call.57
  1759.6 9.7 cholesky.498
  1771.3 8.2 custom-call.59
  1789.5 8.8 cholesky.509
  1799.6 7.4 custom-call.61
  (501 shorter events, 345.6 us)
Async XLA Ops:
  7.2 39.4 %copy-start = (bf16[1,64,3,64,64]{4,3,2,1,0:T(8,128)(2,1)S(1)}, bf16[1,64,3,64,64]{4,3,2,1,0:T(8,128)(2,1)}, u32[]{:S(2)}) copy-start(bf16[1,64,3,64,64]{4,3,2,1,0:T(8,128)(2,1)} %param.26) | copy-start | bytes 4718596
  8.2 516.8 %copy-start.48 = (s32[192]{0:T(256)}, s32[192]{0:T(256)S(1)}, u32[]{:S(2)}) copy-start(s32[192]{0:T(256)S(1)} %eq.37) | copy-start | bytes 2308
  11.1 3.0 copy-start.57
  14.4 32.2 %copy-start.54 = (f32[192]{0:T(256)}, f32[192]{0:T(256)S(1)}, u32[]{:S(2)}) copy-start(f32[192]{0:T(256)S(1)} %convert_element_type.19) | copy-start | bytes 2308
  27.0 76.3 %all-to-all-start.1 = ((f32[64,1,4608]{2,1,0:T(1,128)}), f32[64,1,4608]{2,1,0:T(1,128)}, u32[]{:S(2)}, u32[]{:S(2)}) async-start(f32[64,1,4608]{2,1,0:T(1,128)} %all_to_all.49), calls=%async_computation.1 | async-start | bytes 2359296 | tf_op jit(solution)/shard_map/all_to_all | solution.py:62
  57.7 56.3 %copy-start.58 = (s32[8]{0:T(128)S(1)}, s32[8]{0:T(128)}, u32[]{:S(2)}) copy-start(s32[8]{0:T(128)} %param.25) | copy-start | bytes 100
  57.7 56.4 %copy-start.31 = (f32[12,512]{1,0:T(8,128)S(1)}, f32[12,512]{1,0:T(8,128)}, u32[]{:S(2)}) copy-start(f32[12,512]{1,0:T(8,128)} %param.18) | copy-start | bytes 73732
  57.7 73.7 %copy-start.11 = (bf16[8,64,64]{2,1,0:T(8,128)(2,1)S(1)}, bf16[8,64,64]{2,1,0:T(8,128)(2,1)}, u32[]{:S(2)}) copy-start(bf16[8,64,64]{2,1,0:T(8,128)(2,1)} %param.20) | copy-start | bytes 196612
  103.3 65.9 %all-to-all-start = ((f32[64,1,4608]{2,1,0:T(1,128)}), f32[64,1,4608]{2,1,0:T(1,128)}, u32[]{:S(2)}, u32[]{:S(2)}) async-start(f32[64,1,4608]{2,1,0:T(1,128)} %all_to_all.48), calls=%async_computation | async-start | bytes 2359296 | tf_op jit(solution)/shard_map/all_to_all | solution.py:61
  114.0 481.8 %copy-start.52 = (f32[8,4]{0,1:T(4,128)}, f32[8,4]{0,1:T(4,128)S(1)}, u32[]{:S(2)}) copy-start(f32[8,4]{0,1:T(4,128)S(1)} %fusion.359) | copy-start | bytes 388
  114.1 479.4 %copy-start.43 = (f32[8,4]{1,0:T(8,128)}, f32[8,4]{1,0:T(8,128)S(1)}, u32[]{:S(2)}) copy-start(f32[8,4]{1,0:T(8,128)S(1)} %copy.351) | copy-start | bytes 388
  131.4 5.4 copy-start.45
  135.4 2.6 copy-start.4
  135.4 5.0 copy-start.13
  136.9 4.5 copy-start.30
  149.8 2.8 copy-start.5
  149.8 2.8 copy-start.27
  149.8 2.8 copy-start.29
  177.2 2.8 copy-start.3
  177.2 2.8 copy-start.25
  177.2 2.8 copy-start.28
  180.7 329.6 %copy-start.33 = (f32[1,12,512]{2,1,0:T(8,128)S(1)}, f32[1,12,512]{2,1,0:T(8,128)}, u32[]{:S(2)}) copy-start(f32[1,12,512]{2,1,0:T(8,128)} %reshape.261) | copy-start | bytes 73732
  525.0 4.4 copy-start.55
  540.0 40.0 %all-to-all-start.2 = ((f32[64,1,2304]{2,1,0:T(1,128)}), f32[64,1,2304]{2,1,0:T(1,128)}, u32[]{:S(2)}, u32[]{:S(2)}) async-start(f32[64,1,2304]{2,1,0:T(1,128)} %all_to_all.50), calls=%async_computation.2 | async-start | bytes 1179648 | tf_op jit(solution)/shard_map/all_to_all | solution.py:61
  556.8 3.6 copy-start.32
  556.8 3.6 copy-start.47
  562.8 34.2 %copy-start.12 = (bf16[8,64,64]{2,1,0:T(8,128)(2,1)S(1)}, bf16[8,64,64]{2,1,0:T(8,128)(2,1)}, u32[]{:S(2)}) copy-start(bf16[8,64,64]{2,1,0:T(8,128)(2,1)} %param.20) | copy-start | bytes 196612
  580.1 49.1 %all-to-all-start.3 = ((f32[64,1,2304]{2,1,0:T(1,128)}), f32[64,1,2304]{2,1,0:T(1,128)}, u32[]{:S(2)}, u32[]{:S(2)}) async-start(f32[64,1,2304]{2,1,0:T(1,128)} %all_to_all.51), calls=%async_computation.3 | async-start | bytes 1179648 | tf_op jit(solution)/shard_map/all_to_all | solution.py:62
  587.6 320.0 %all-reduce.11.cloned.1.call-start = ((), (), s32[]{:S(2)}) async-start(), calls=%async_computation.7 | async-start | bytes 294912 | tf_op jit(solution)/shard_map/psum | solution.py:89
  593.5 6.2 copy-start.26
  619.2 4.8 copy-start.38
  619.2 4.8 copy-start.41
  621.8 3.9 copy-start.20
  629.2 5.9 copy-start.49
  635.0 4.0 copy-start.19
  947.0 0.8 copy-start.15
  947.7 57.5 %copy-start.61 = (s32[2]{0:T(128)S(1)}, s32[2]{0:T(128)}, u32[]{:S(2)}) copy-start(s32[2]{0:T(128)} %iota_multiply_fusion) | copy-start | bytes 28
  960.3 51.5 %copy-start.17 = (f32[128,96]{1,0:T(8,128)S(1)}, f32[128,96]{1,0:T(8,128)}, u32[]{:S(2)}) copy-start(f32[128,96]{1,0:T(8,128)} %pad_convert_fusion) | copy-start | bytes 147460
  1005.2 0.8 copy-start.7
  1066.5 0.8 copy-start.1
  1141.0 12.7 copy-start.16
  1169.8 0.6 copy-start.35
  1185.4 5.1 copy-start.56
  1201.1 42.7 %all-to-all-start.4 = ((f32[64,1,2304]{2,1,0:T(1,128)}), f32[64,1,2304]{2,1,0:T(1,128)}, u32[]{:S(2)}, u32[]{:S(2)}) async-start(f32[64,1,2304]{2,1,0:T(1,128)} %all_to_all.52), calls=%async_computation.4 | async-start | bytes 1179648 | tf_op jit(solution)/shard_map/all_to_all | solution.py:61
  1220.8 3.0 copy-start.44
  1220.8 4.4 copy-start.46
  1223.8 3.7 copy-start.10
  1228.7 26.5 %copy-start.53 = (f32[8,4]{0,1:T(4,128)S(1)}, f32[8,4]{0,1:T(4,128)}, u32[]{:S(2)}) copy-start(f32[8,4]{0,1:T(4,128)} %copy-done.52) | copy-start | bytes 388
  1243.7 43.8 %all-to-all-start.5 = ((f32[64,1,2304]{2,1,0:T(1,128)}), f32[64,1,2304]{2,1,0:T(1,128)}, u32[]{:S(2)}, u32[]{:S(2)}) async-start(f32[64,1,2304]{2,1,0:T(1,128)} %all_to_all.53), calls=%async_computation.5 | async-start | bytes 1179648 | tf_op jit(solution)/shard_map/all_to_all | solution.py:62
  1251.3 302.2 %all-reduce.9.cloned.1.call-start = ((), (), s32[]{:S(2)}) async-start(), calls=%async_computation.6 | async-start | bytes 294912 | tf_op jit(solution)/shard_map/psum | solution.py:89
  1252.8 7.2 copy-start.8
  1252.8 8.2 copy-start.9
  1277.7 5.9 copy-start.50
  1281.0 4.8 copy-start.37
  1281.0 4.8 copy-start.40
  1287.5 5.9 copy-start.51
  1290.8 4.8 copy-start.39
  1293.4 3.9 copy-start.36
  1293.4 6.5 copy-start.34
  1592.8 0.8 copy-start.14
  1593.6 58.8 %copy-start.60 = (s32[2,2]{1,0:T(2,128)S(1)}, s32[2,2]{1,0:T(2,128)}, u32[]{:S(2)}) copy-start(s32[2,2]{1,0:T(2,128)} %copy-done.59) | copy-start | bytes 52
  1606.1 52.1 %copy-start.18 = (f32[128,96]{1,0:T(8,128)S(1)}, f32[128,96]{1,0:T(8,128)}, u32[]{:S(2)}) copy-start(f32[128,96]{1,0:T(8,128)} %pad_convert_fusion) | copy-start | bytes 147460
  1651.6 0.8 copy-start.6
  1712.5 0.8 copy-start.2
  (6 other events, 3.7 us)
Sparse Core Ops, SparseCore 0:
  657.0 250.5 all-reduce.10
  1302.6 250.8 all-reduce.8
where the time goes:
time: 1840 us; the launch traced here: 1820 us
  waiting for transfers between devices  573 us (31%)
  blocking collectives  487 us (26%)
  other arithmetic  339 us (18%)
  matrix products  201 us (11%)
  local copies, waits for them, and re-layouts  144 us (8%)
  starting transfers between devices  60.1 us (3%)
  between operations  19.9 us (1%)
    psum x2, waiting for transfers between devices, gram_pair(): summed_k, summed_m = lax.psum((part_k, part_m), 'rows')  483 us
    psum x1, blocking collectives, gram_pair(): summed_k, summed_m = lax.psum((part_k, part_m), 'rows')  223 us
    all_gather x3, blocking collectives, gram_pair(): lax.all_gather(summed_m, 'cols', axis=3, tiled=True)  100 us
    another operation x21, other arithmetic, rayleigh(): factor = jnp.linalg.cholesky(gram_stiff)  98.4 us
    all_gather x3, blocking collectives, gram_pair(): lax.all_gather(summed_k, 'cols', axis=3, tiled=True)  62.8 us
    another operation x11, other arithmetic, rayleigh(): jax.scipy.linalg.cho_solve((factor, True), jnp.dot(gram_mass, coeffs, pre...  62.4 us
    another operation x18, other arithmetic, rayleigh(): inner_factor = jnp.linalg.cholesky(inner)  60.2 us
    another operation x12, other arithmetic, rayleigh(): jax.scipy.linalg.solve_triangular(inner_factor, solved.T, lower=True)  53.7 us
  transfers between devices with their start and end apart: 8, of which 6 were waited for; matrix products, arithmetic and copies ran while one was open for 6% of the time, Pallas kernels for 0%

commit v1 on v0

--- a/solution.py
+++ b/solution.py
@@ -80,7 +80,9 @@
     modes = col_part * lax.axis_size("cols")
     dof_count = row_count * lax.axis_size("rows")
     empty = jnp.zeros((blocks, modes, blocks, col_part), jnp.float32)
-    panel_rows = lax.all_gather(own_s, "cols", axis=1, tiled=True)
+    panel_rows = jnp.concatenate(
+        lax.all_to_all(jnp.stack([own_s] * lax.axis_size("cols")), "cols", 0, 0), axis=1
+    )
     offset = jnp.int32(0)
     term_k = jnp.einsum("anr,bcr->anbc", panel_rows, own_k, precision=exact_dots)
     term_m = jnp.einsum("anr,bcr->anbc", panel_rows, own_m, precision=exact_dots)

time: 1840 us -> 1850 us (level)
    psum x2, waiting for transfers between devices: 483 us -> 453 us  [gram_pair(): summed_k, summed_m = lax.psum((part_k, part_m), 'rows')]
    all_to_all x0 -> x3, starting transfers between devices: none -> 18.9 us  [gram_pair(): lax.all_to_all(jnp.stack([own_s] * lax.axis_size('cols')), 'cols', 0, 0)]
    all_gather x3 -> x2, blocking collectives: 47.5 us -> 33.1 us  [body(): panel_rows = lax.all_gather(own_s, 'cols', axis=1, tiled=True)]
  transfers between devices with their start and end apart: 8 -> 11, of which waited for: 6 -> 8; matrix products, arithmetic and copies ran while one was open for 6% -> 9% of each run, Pallas kernels for 0% -> 0%
where the time goes in v1:
time: 1850 us; the launch traced here: 1830 us
  waiting for transfers between devices  562 us (30%)
  blocking collectives  475 us (26%)
  other arithmetic  342 us (18%)
  matrix products  202 us (11%)
  local copies, waits for them, and re-layouts  151 us (8%)
  starting transfers between devices  77.9 us (4%)
  between operations  20.2 us (1%)
    psum x2, waiting for transfers between devices, gram_pair(): summed_k, summed_m = lax.psum((part_k, part_m), 'rows')  453 us
    psum x1, blocking collectives, gram_pair(): summed_k, summed_m = lax.psum((part_k, part_m), 'rows')  222 us
    all_gather x3, blocking collectives, gram_pair(): lax.all_gather(summed_m, 'cols', axis=3, tiled=True)  100 us
    another operation x21, other arithmetic, rayleigh(): factor = jnp.linalg.cholesky(gram_stiff)  97.9 us
    all_gather x3, blocking collectives, gram_pair(): lax.all_gather(summed_k, 'cols', axis=3, tiled=True)  63.4 us
    another operation x11, other arithmetic, rayleigh(): jax.scipy.linalg.cho_solve((factor, True), jnp.dot(gram_mass, coeffs, pre...  62.5 us
    all_to_all x3, waiting for transfers between devices, apply_pair(): lax.all_to_all(face_term(m_faces), 'rows', split_axis=0, concat_axis=0, t...  61.7 us
    another operation x18, other arithmetic, rayleigh(): inner_factor = jnp.linalg.cholesky(inner)  60.4 us
  transfers between devices with their start and end apart: 11, of which 8 were waited for; matrix products, arithmetic and copies ran while one was open for 9% of the time, Pallas kernels for 0%

profile of v1, /device:TPU:1, one launch (start us, length us, event | category | flops | bytes accessed | tf_op | source)
XLA Modules:
  0.0 1831.2 jit_solution(13353500352175629495)
XLA Ops:
  8.9 10.2 all-to-all-start.2
  26.1 9.0 convolution_multiply_fusion
  35.1 3.7 all_to_all.61
  38.8 14.5 all-to-all-start.1
  53.4 7.4 convolution_multiply_fusion.1
  64.4 48.1 %all-to-all-done.1 = f32[64,1,4608]{2,1,0:T(1,128)} async-done(((f32[64,1,4608]{2,1,0:T(1,128)}), f32[64,1,4608]{2,1,0:T(1,128)}, u32[]{:S(2)}, u32[]{:S(2)}) %all-to-all-start.1) | async-done | bytes 1179680 | tf_op jit(solution)/shard_map/all_to_all | solution.py:62
  112.5 7.3 all-to-all-start
  134.7 5.1 reduce.17
  150.4 25.8 %all-to-all-done = f32[64,1,4608]{2,1,0:T(1,128)} async-done(((f32[64,1,4608]{2,1,0:T(1,128)}), f32[64,1,4608]{2,1,0:T(1,128)}, u32[]{:S(2)}, u32[]{:S(2)}) %all-to-all-start) | async-done | bytes 1179680 | tf_op jit(solution)/shard_map/all_to_all | solution.py:61
  176.2 5.1 reduce.16
  191.3 222.1 %all-reduce.5 = (f32[1,96,1,12]{1,3,2,0:T(8,128)S(1)}, f32[1,96,1,12]{1,3,2,0:T(8,128)S(1)}) all-reduce(f32[1,96,1,12]{1,3,2,0:T(8,128)S(1)} %convolution_bitcast_fusion.19, f32[1,96,1,12]{1,3,2,0:T(8,128)S(1)} %convolution_bitcast_fusion.20), channel_id=1, replica_groups=mesh['rows'=64,'cols'=8] {'rows'}, use_global_device_ids=true, to_apply=%region_3.5 | all-reduce | flops 2304 | bytes 18432 | tf_op jit(solution)/shard_map/psum | solution.py:91
  413.4 71.6 %all_gather.36 = f32[1,96,1,96]{1,2,0,3:T(1,128)S(1)} all-gather(f32[1,96,1,12]{1,2,0,3:T(1,128)S(1)} %copy.369), channel_id=1, replica_groups=mesh['rows'=64,'cols'=8] {'cols'}, dimensions={3}, use_global_device_ids=true | all-gather | bytes 41472 | tf_op jit(solution)/shard_map/all_gather | solution.py:94
  485.4 8.8 cholesky.329
  495.5 7.4 custom-call.31
  502.9 12.8 all_gather.37
  517.1 12.8 all-gather
  533.6 4.5 all-to-all-start.3
  542.5 7.6 convolution_multiply_fusion.5
  553.2 6.2 all-to-all-start.4
  562.8 8.5 convolution_multiply_fusion.4
  575.1 14.5 all_gather.41
  592.9 13.8 all-to-all-start.5
  633.4 6.9 all-to-all-done.5
  653.4 17.2 all_gather.42
  670.6 13.4 all_gather.43
  687.1 225.0 %all-reduce.11.cloned.1.call-done = (f32[3,96,3,12]{1,3,2,0:T(8,128)}, f32[3,96,3,12]{1,3,2,0:T(8,128)}) async-done(((f32[3,96,3,12]{1,3,2,0:T(8,128)}, f32[3,96,3,12]{1,3,2,0:T(8,128)}), (f32[3,96,3,12]{1,3,2,0:T(8,128)}, f32[3,96,3,12]{1,3,2,0:T(8,128)})) %all-reduce.11.cloned.1.call-update) | async-done | bytes 82960 | tf_op jit(solution)/shard_map/psum | solution.py:91
  913.0 25.3 %all_gather.39 = f32[3,96,3,96]{1,2,0,3:T(4,128)} all-gather(f32[3,96,3,12]{1,2,0,3:T(4,128)S(1)} %copy.396), channel_id=1, replica_groups=mesh['rows'=64,'cols'=8] {'cols'}, dimensions={3}, use_global_device_ids=true | all-gather | bytes 373248 | tf_op jit(solution)/shard_map/all_gather | solution.py:93
  952.6 11.7 cholesky.342
  965.1 9.8 custom-call.46
  977.9 11.7 cholesky.361
  990.2 10.0 custom-call.47
  1010.6 5.8 while.12
  1016.9 29.5 %custom-call.52 = f32[3,128,128]{1,2,0:T(8,128)S(1)} custom-call(f32[3,128,128]{2,1,0:T(8,128)S(1)} %pad_maximum_fusion), custom_call_target="InvertDiagBlocksLowerTriangular" | custom-call | tf_op jit(solution)/shard_map/jit(_cho_solve)/triangular_solve | solution.py:109
  1047.4 14.3 all_gather.40
  1084.5 9.6 cholesky.397
  1096.0 8.2 custom-call.49
  1118.3 10.0 cholesky.408
  1130.2 8.2 custom-call.51
  1148.4 8.8 cholesky.419
  1158.5 7.4 custom-call.53
  1181.0 13.0 all-gather.1
  1197.8 4.3 all-to-all-start.6
  1206.5 7.5 convolution_multiply_fusion.3
  1217.1 9.1 all-to-all-start.7
  1227.5 8.5 convolution_multiply_fusion.2
  1239.0 20.7 %all-to-all-done.7 = f32[64,1,2304]{2,1,0:T(1,128)} async-done(((f32[64,1,2304]{2,1,0:T(1,128)}), f32[64,1,2304]{2,1,0:T(1,128)}, u32[]{:S(2)}, u32[]{:S(2)}) %all-to-all-start.7) | async-done | bytes 589856 | tf_op jit(solution)/shard_map/all_to_all | solution.py:61
  1259.7 7.5 all-to-all-start.8
  1292.2 6.7 all-to-all-done.8
  1313.5 18.6 %all_gather.47 = f32[3,96,512]{2,0,1:T(4,128)S(1)} all-gather(f32[3,12,512]{2,0,1:T(4,128)S(1)} %copy-done.27), channel_id=1, replica_groups=mesh['rows'=64,'cols'=8] {'cols'}, dimensions={1}, use_global_device_ids=true | all-gather | bytes 663552 | tf_op jit(solution)/shard_map/all_gather | solution.py:206
  1333.2 227.7 %all-reduce.9.cloned.1.call-done = (f32[3,96,3,12]{1,3,2,0:T(8,128)}, f32[3,96,3,12]{1,3,2,0:T(8,128)}) async-done(((f32[3,96,3,12]{1,3,2,0:T(8,128)}, f32[3,96,3,12]{1,3,2,0:T(8,128)}), (f32[3,96,3,12]{1,3,2,0:T(8,128)}, f32[3,96,3,12]{1,3,2,0:T(8,128)})) %all-reduce.9.cloned.1.call-update) | async-done | bytes 82960 | tf_op jit(solution)/shard_map/psum | solution.py:91
  1561.8 25.3 %all_gather.45 = f32[3,96,3,96]{1,2,0,3:T(4,128)} all-gather(f32[3,96,3,12]{1,2,0,3:T(4,128)S(1)} %copy.454), channel_id=1, replica_groups=mesh['rows'=64,'cols'=8] {'cols'}, dimensions={3}, use_global_device_ids=true | all-gather | bytes 373248 | tf_op jit(solution)/shard_map/all_gather | solution.py:93
  1601.4 11.7 cholesky.432
  1614.0 9.8 custom-call.54
  1626.7 11.7 cholesky.451
  1640.3 9.9 custom-call.55
  1660.0 5.8 while.13
  1665.9 29.5 %custom-call.60 = f32[3,128,128]{1,2,0:T(8,128)S(1)} custom-call(f32[3,128,128]{2,1,0:T(8,128)S(1)} %pad_maximum_fusion.1), custom_call_target="InvertDiagBlocksLowerTriangular" | custom-call | tf_op jit(solution)/shard_map/jit(_cho_solve)/triangular_solve | solution.py:109
  1696.4 14.3 all_gather.46
  1733.5 9.6 cholesky.487
  1745.0 8.2 custom-call.57
  1767.3 9.8 cholesky.498
  1779.0 8.2 custom-call.59
  1797.2 8.8 cholesky.509
  1807.3 7.4 custom-call.61
  (524 shorter events, 369.8 us)
Async XLA Ops:
  7.2 46.2 %copy-start = (bf16[1,64,3,64,64]{4,3,2,1,0:T(8,128)(2,1)S(1)}, bf16[1,64,3,64,64]{4,3,2,1,0:T(8,128)(2,1)}, u32[]{:S(2)}) copy-start(bf16[1,64,3,64,64]{4,3,2,1,0:T(8,128)(2,1)} %param.26) | copy-start | bytes 4718596
  8.9 29.9 %all-to-all-start.2 = ((f32[8,1,12,512]{3,1,2,0:T(1,128)}), f32[8,1,12,512]{3,1,2,0:T(1,128)S(1)}, u32[]{:S(2)}, u32[]{:S(2)}) async-start(f32[8,1,12,512]{3,1,2,0:T(1,128)} %stack.82), calls=%async_computation.2 | async-start | bytes 393216 | tf_op jit(solution)/shard_map/all_to_all | solution.py:84
  19.9 164.7 %copy-start.52 = (s32[192]{0:T(256)}, s32[192]{0:T(256)S(1)}, u32[]{:S(2)}) copy-start(s32[192]{0:T(256)S(1)} %eq.37) | copy-start | bytes 2308
  22.8 3.0 copy-start.62
  26.1 27.3 %copy-start.59 = (f32[192]{0:T(256)}, f32[192]{0:T(256)S(1)}, u32[]{:S(2)}) copy-start(f32[192]{0:T(256)S(1)} %convert_element_type.19) | copy-start | bytes 2308
  38.8 22.0 %copy-start.17 = (f32[8,1,12,512]{3,1,2,0:T(1,128)}, f32[8,1,12,512]{3,1,2,0:T(1,128)S(1)}, u32[]{:S(2)}) copy-start(f32[8,1,12,512]{3,1,2,0:T(1,128)S(1)} %all-to-all-done.2) | copy-start | bytes 589828
  38.8 73.7 %all-to-all-start.1 = ((f32[64,1,4608]{2,1,0:T(1,128)}), f32[64,1,4608]{2,1,0:T(1,128)}, u32[]{:S(2)}, u32[]{:S(2)}) async-start(f32[64,1,4608]{2,1,0:T(1,128)} %all_to_all.61), calls=%async_computation.1 | async-start | bytes 2359296 | tf_op jit(solution)/shard_map/all_to_all | solution.py:62
  64.4 56.1 %copy-start.63 = (s32[8]{0:T(128)S(1)}, s32[8]{0:T(128)}, u32[]{:S(2)}) copy-start(s32[8]{0:T(128)} %param.25) | copy-start | bytes 100
  64.4 56.2 %copy-start.11 = (bf16[8,64,64]{2,1,0:T(8,128)(2,1)S(1)}, bf16[8,64,64]{2,1,0:T(8,128)(2,1)}, u32[]{:S(2)}) copy-start(bf16[8,64,64]{2,1,0:T(8,128)(2,1)} %param.20) | copy-start | bytes 196612
  112.5 63.7 %all-to-all-start = ((f32[64,1,4608]{2,1,0:T(1,128)}), f32[64,1,4608]{2,1,0:T(1,128)}, u32[]{:S(2)}, u32[]{:S(2)}) async-start(f32[64,1,4608]{2,1,0:T(1,128)} %all_to_all.60), calls=%async_computation | async-start | bytes 2359296 | tf_op jit(solution)/shard_map/all_to_all | solution.py:61
  120.6 10.0 copy-start.57
  120.7 6.5 copy-start.45
  120.7 5.4 copy-start.48
  124.6 5.0 copy-start.13
  126.1 4.5 copy-start.32
  142.7 2.8 copy-start.6
  142.7 2.8 copy-start.29
  142.7 2.8 copy-start.31
  184.7 2.8 copy-start.3
  184.7 2.8 copy-start.28
  184.7 2.8 copy-start.30
  188.1 328.9 %copy-start.34 = (f32[1,12,512]{2,1,0:T(8,128)S(1)}, f32[1,12,512]{2,1,0:T(8,128)}, u32[]{:S(2)}) copy-start(f32[1,12,512]{2,1,0:T(8,128)} %reshape.282) | copy-start | bytes 73732
  190.0 341.8 %copy-start.33 = (f32[12,512]{1,0:T(8,128)S(1)}, f32[12,512]{1,0:T(8,128)}, u32[]{:S(2)}) copy-start(f32[12,512]{1,0:T(8,128)} %param.18) | copy-start | bytes 73732
  530.6 7.5 copy-start.53
  533.6 19.6 %all-to-all-start.3 = ((f32[8,3,12,512]{3,2,1,0:T(8,128)}), f32[8,3,12,512]{3,2,1,0:T(8,128)}, u32[]{:S(2)}, u32[]{:S(2)}) async-start(f32[8,3,12,512]{3,2,1,0:T(8,128)} %stack.86), calls=%async_computation.3 | async-start | bytes 1572864 | tf_op jit(solution)/shard_map/all_to_all | solution.py:84
  538.1 4.4 copy-start.60
  550.1 11.9 copy-start.43
  553.2 39.8 %all-to-all-start.4 = ((f32[64,1,2304]{2,1,0:T(1,128)}), f32[64,1,2304]{2,1,0:T(1,128)}, u32[]{:S(2)}, u32[]{:S(2)}) async-start(f32[64,1,2304]{2,1,0:T(1,128)} %all_to_all.62), calls=%async_computation.4 | async-start | bytes 1179648 | tf_op jit(solution)/shard_map/all_to_all | solution.py:61
  571.3 3.0 copy-start.42
  574.4 16.2 copy-start.46
  575.1 15.5 copy-start.4
  589.6 18.0 copy-start.51
  589.6 18.6 %copy-start.49 = (s32[8,4]{0,1:T(4,128)S(1)}, s32[8,4]{0,1:T(4,128)}, u32[]{:S(2)}) copy-start(s32[8,4]{0,1:T(4,128)} %param.24) | copy-start | bytes 388
  591.6 21.8 %copy-start.12 = (bf16[8,64,64]{2,1,0:T(8,128)(2,1)S(1)}, bf16[8,64,64]{2,1,0:T(8,128)(2,1)}, u32[]{:S(2)}) copy-start(bf16[8,64,64]{2,1,0:T(8,128)(2,1)} %param.20) | copy-start | bytes 196612
  592.9 47.4 %all-to-all-start.5 = ((f32[64,1,2304]{2,1,0:T(1,128)}), f32[64,1,2304]{2,1,0:T(1,128)}, u32[]{:S(2)}, u32[]{:S(2)}) async-start(f32[64,1,2304]{2,1,0:T(1,128)} %all_to_all.63), calls=%async_computation.5 | async-start | bytes 1179648 | tf_op jit(solution)/shard_map/all_to_all | solution.py:62
  606.7 305.4 %all-reduce.11.cloned.1.call-start = ((), (), s32[]{:S(2)}) async-start(), calls=%async_computation.10 | async-start | bytes 294912 | tf_op jit(solution)/shard_map/psum | solution.py:91
  623.6 4.9 copy-start.39
  623.6 4.9 copy-start.41
  626.3 3.9 copy-start.22
  633.4 12.7 copy-start.54
  646.2 4.0 copy-start.21
  952.6 57.2 %copy-start.66 = (s32[2]{0:T(128)S(1)}, s32[2]{0:T(128)}, u32[]{:S(2)}) copy-start(s32[2]{0:T(128)} %iota_multiply_fusion) | copy-start | bytes 28
  965.1 51.2 %copy-start.19 = (f32[128,96]{1,0:T(8,128)S(1)}, f32[128,96]{1,0:T(8,128)}, u32[]{:S(2)}) copy-start(f32[128,96]{1,0:T(8,128)} %pad_convert_fusion) | copy-start | bytes 147460
  1145.9 12.7 copy-start.18
  1194.7 7.3 copy-start.55
  1197.8 19.3 %all-to-all-start.6 = ((f32[8,3,12,512]{3,2,1,0:T(8,128)}), f32[8,3,12,512]{3,2,1,0:T(8,128)}, u32[]{:S(2)}, u32[]{:S(2)}) async-start(f32[8,3,12,512]{3,2,1,0:T(8,128)} %stack.95), calls=%async_computation.6 | async-start | bytes 1572864 | tf_op jit(solution)/shard_map/all_to_all | solution.py:84
  1202.0 4.5 copy-start.61
  1217.1 42.7 %all-to-all-start.7 = ((f32[64,1,2304]{2,1,0:T(1,128)}), f32[64,1,2304]{2,1,0:T(1,128)}, u32[]{:S(2)}, u32[]{:S(2)}) async-start(f32[64,1,2304]{2,1,0:T(1,128)} %all_to_all.64), calls=%async_computation.7 | async-start | bytes 1179648 | tf_op jit(solution)/shard_map/all_to_all | solution.py:61
  1236.0 31.5 %copy-start.47 = (f32[8,4]{1,0:T(8,128)S(1)}, f32[8,4]{1,0:T(8,128)}, u32[]{:S(2)}) copy-start(f32[8,4]{1,0:T(8,128)} %copy-done.45) | copy-start | bytes 388
  1236.0 33.0 %copy-start.50 = (s32[8,4]{0,1:T(4,128)S(1)}, s32[8,4]{0,1:T(4,128)}, u32[]{:S(2)}) copy-start(s32[8,4]{0,1:T(4,128)} %param.24) | copy-start | bytes 388
  1239.0 33.2 %copy-start.58 = (f32[8,4]{0,1:T(4,128)S(1)}, f32[8,4]{0,1:T(4,128)}, u32[]{:S(2)}) copy-start(f32[8,4]{0,1:T(4,128)} %copy-done.57) | copy-start | bytes 388
  1259.7 39.1 %all-to-all-start.8 = ((f32[64,1,2304]{2,1,0:T(1,128)}), f32[64,1,2304]{2,1,0:T(1,128)}, u32[]{:S(2)}, u32[]{:S(2)}) async-start(f32[64,1,2304]{2,1,0:T(1,128)} %all_to_all.65), calls=%async_computation.8 | async-start | bytes 1179648 | tf_op jit(solution)/shard_map/all_to_all | solution.py:62
  1267.2 293.7 %all-reduce.9.cloned.1.call-start = ((), (), s32[]{:S(2)}) async-start(), calls=%async_computation.9 | async-start | bytes 294912 | tf_op jit(solution)/shard_map/psum | solution.py:91
  1267.5 7.7 copy-start.14
  1267.5 8.6 copy-start.9
  1267.5 9.6 copy-start.10
  1282.3 5.9 copy-start.56
  1285.6 4.8 copy-start.38
  1285.6 4.8 copy-start.40
  1304.7 4.0 copy-start.37
  1304.7 6.4 copy-start.35
  1306.9 6.6 copy-start.27
  1601.4 58.6 %copy-start.65 = (s32[2,2]{1,0:T(2,128)S(1)}, s32[2,2]{1,0:T(2,128)}, u32[]{:S(2)}) copy-start(s32[2,2]{1,0:T(2,128)} %copy-done.64) | copy-start | bytes 52
  1614.0 51.8 %copy-start.20 = (f32[128,96]{1,0:T(8,128)S(1)}, f32[128,96]{1,0:T(8,128)}, u32[]{:S(2)}) copy-start(f32[128,96]{1,0:T(8,128)} %pad_convert_fusion) | copy-start | bytes 147460
  (14 other events, 11.5 us)
Sparse Core Ops, SparseCore 0:
  670.7 241.4 all-reduce.10
  1313.6 247.2 all-reduce.8
